TPU v7x, 32 devices: a whole 2x2x4 slice. The times are simulated.
32 devices in a mesh: seq: 2 (over y), dom: 8 (over z, x), tm: 2 (over core).
Axes of the slice: x: 2, y: 2, z: 4, core: 2. Of those that a mesh axis runs over, the one named last changes fastest.
Arguments:
- particles: bfloat16 [4, 1536, 128], P('tm', ('seq', 'dom')), parts along dimension 1, may hold values from -6 to 6
- log_weight: float32 [4, 1536], P('tm', ('seq', 'dom')), parts along dimension 1, may hold values from -13 to 313
- trans_weight: bfloat16 [128, 128], replicated, may hold values from -0.5 to 0.5
- precision: float32 [128], replicated, may hold values from 0.2 to 2
Outputs:
- smoothed: float32 [4, 1536], P('tm', ('seq', 'dom')), parts along dimension 1
- score: float32 [256, 128], P('seq'), parts along dimension 0
There are 2 independent parts, one for each index of `seq`. A program takes and returns all parts, laid end to end along the dimension named above; an argument that names none is the same for every part. Nothing has to cross between parts.
All inputs are finite; a program needn't handle non-finite values.
Results may differ from a plain program's by a relative error of at most 0.0061.
Values may be sent and summed in bfloat16 or wider, within the bound.
A program may use at most 64 MiB of HBM per device.

v0:
```python
import jax
import jax.numpy as jnp
from jax import lax
from jax.sharding import PartitionSpec as P

exact_mode = lax.Precision.HIGHEST


def from_behind(x, axis, by):
    size = lax.axis_size(axis)
    pairs = [(i, i + by) for i in range(size) if 0 <= i + by < size]
    return lax.ppermute(x, axis, pairs)


def block_size(length):
    best = 1
    for trial in range(1, min(length, 512) + 1):
        if length % trial == 0:
            best = trial
    return best


def project_rows(rows, precision, weight_full):
    return jnp.dot(rows.astype(jnp.float32) * precision, weight_full, precision=exact_mode).astype(
        jnp.bfloat16
    )


def pair_scores(row_proj, column_rows, column_bias):
    return (
        jnp.einsum("id,jd->ij", row_proj, column_rows, preferred_element_type=jnp.float32)
        + column_bias[None, :]
    )


def make_norm_fold(row_proj, bias_row, carried, block_in, first_row):
    length = block_in.shape[0]
    size = block_size(length)

    def inner(position, state):
        row_top, row_total = state
        offset = position * size
        column_rows = lax.dynamic_slice_in_dim(block_in, offset, size, 0)
        bias_part = lax.dynamic_slice_in_dim(bias_row, first_row + offset, size, 0)
        scores = pair_scores(row_proj, column_rows, bias_part)
        new_top = jnp.maximum(row_top, jnp.max(scores, axis=1))
        row_total = row_total * jnp.exp(row_top - new_top) + jnp.sum(
            jnp.exp(scores - new_top[:, None]), axis=1
        )
        return (new_top, row_total)

    return lax.fori_loop(0, length // size, inner, carried)


def make_column_fold(row_proj, bias_row, row_norm, row_weight, carried, block_in, first_row):
    length = block_in.shape[0]
    size = block_size(length)

    def inner(position, state):
        moved, column_sums = state
        offset = position * size
        column_rows = lax.dynamic_slice_in_dim(block_in, offset, size, 0)
        bias_part = lax.dynamic_slice_in_dim(bias_row, first_row + offset, size, 0)
        scores = pair_scores(row_proj, column_rows, bias_part)
        backward = (row_weight[:, None] * jnp.exp(scores - row_norm[:, None])).astype(jnp.bfloat16)
        moved = moved + jnp.dot(backward, column_rows, preferred_element_type=jnp.float32)
        column_sums = lax.dynamic_update_slice_in_dim(
            column_sums, jnp.sum(backward.astype(jnp.float32), axis=0), first_row + offset, 0
        )
        return (moved, column_sums)

    return lax.fori_loop(0, length // size, inner, carried)


def shards(particles, log_weight, trans_weight, precision):
    steps_here, rows_here, width = particles.shape
    tm_count = lax.axis_size("tm")
    dom_count = lax.axis_size("dom")
    total_rows = rows_here * dom_count
    tm_place = lax.axis_index("tm")
    is_last = tm_place == tm_count - 1
    weight_full = trans_weight.astype(jnp.float32)
    boundary = from_behind(particles[0], "tm", -1)
    later_sets = [particles[1]] + [boundary]
    later_proj = [project_rows(rows, precision, weight_full) for rows in later_sets]
    biases = []
    for k in range(steps_here):
        predicted = jnp.dot(particles[k], trans_weight.T, preferred_element_type=jnp.float32)
        biases.append(log_weight[k] - 0.5 * jnp.sum(precision * predicted * predicted, axis=1))
    local_bias = jnp.stack(biases)
    full_bias = lax.all_gather(local_bias, "dom", axis=1, tiled=True)
    row_norms = []
    whole = lax.all_gather(particles, "dom", axis=1, tiled=True)
    for k in range(steps_here):
        start_state = (
            jnp.full((rows_here,), -jnp.inf, jnp.float32),
            jnp.zeros((rows_here,), jnp.float32),
        )
        row_top, row_total = make_norm_fold(later_proj[k], full_bias[k], start_state, whole[k], 0)
        row_norms.append(row_top + jnp.log(row_total))
    final_logs = log_weight[steps_here - 1]
    global_top = lax.pmax(jnp.max(final_logs), "dom")
    global_total = lax.psum(jnp.sum(jnp.exp(final_logs - global_top)), "dom")
    final_weights = jnp.exp(final_logs - global_top) / global_total
    carried = (
        jnp.zeros((steps_here, rows_here), jnp.float32),
        jnp.zeros((width, width), jnp.float32),
    )
    for r in range(tm_count):
        if r == 0:
            incoming = jnp.zeros((rows_here,), jnp.float32)
        else:
            incoming = from_behind(carried[0][0], "tm", -1)
        owner = tm_count - 1 - r
        backward_partial_value = jnp.zeros((width, width), jnp.float32)
        outputs = [None] * steps_here
        row_weight = incoming
        for backward_k in range(steps_here - 1, -1, -1):
            column_rows = particles[backward_k]
            backward_start_state = (
                jnp.zeros((rows_here, width), jnp.float32),
                jnp.zeros((total_rows,), jnp.float32),
            )
            moved, column_sums = make_column_fold(
                later_proj[backward_k],
                full_bias[backward_k],
                row_norms[backward_k],
                row_weight,
                backward_start_state,
                whole[backward_k],
                0,
            )
            column_weights = lax.psum_scatter(column_sums, "dom", scatter_dimension=0, tiled=True)
            outer = jnp.dot(
                later_sets[backward_k].astype(jnp.float32).T, moved, precision=exact_mode
            )
            column_float = column_rows.astype(jnp.float32)
            moment = jnp.dot(
                column_float.T * column_weights[None, :], column_float, precision=exact_mode
            )
            backward_partial_value = backward_partial_value + precision[:, None] * (
                outer - jnp.dot(weight_full, moment, precision=exact_mode)
            )
            if backward_k == steps_here - 1:
                column_weights = jnp.where(is_last, final_weights, column_weights)
            outputs[backward_k] = column_weights
            row_weight = column_weights
        is_owner = tm_place == owner
        carried = (
            jnp.where(is_owner, jnp.stack(outputs), carried[0]),
            jnp.where(is_owner, backward_partial_value, carried[1]),
        )
    stacked, partial_value = carried
    score = lax.psum(partial_value, ("dom", "tm"))
    return (stacked * total_rows, score)


def solution(mesh):
    placed = (P("tm", ("seq", "dom"), None), P("tm", ("seq", "dom")), P(), P())
    return jax.shard_map(
        shards,
        mesh=mesh,
        in_specs=placed,
        out_specs=(P("tm", ("seq", "dom")), P("seq", None)),
        check_vma=False,
    )
```

profile of v0, /device:TPU:8, one launch (start us, length us, event | category | flops | bytes accessed | tf_op | source)
XLA Modules:
  0.0 267.3 jit_solution(9784451875654501515)
XLA Ops:
  7.2 0.8 slice_bitcast_fusion.2
  8.0 1.4 collective-permute-start
  9.4 28.6 %all_gather.6 = bf16[2,768,128]{2,1,0:T(8,128)(2,1)S(1)} all-gather(bf16[2,96,128]{2,1,0:T(8,128)(2,1)S(1)} %copy-done.1), channel_id=1, replica_groups=mesh['seq'=2,'dom'=8,'tm'=2] {'dom'}, dimensions={1}, use_global_device_ids=true | all-gather | bytes 442368 | tf_op jit(solution)/shard_map/all_gather | solution.py:93
  38.0 0.3 fusion.54
  38.3 0.3 fusion.53
  38.8 0.6 copy-done.3
  39.4 0.6 slice_reduce_fusion.2
  40.0 22.1 %pmax.7 = f32[]{:T(128)} all-reduce(f32[]{:T(128)} %slice_reduce_fusion.2), channel_id=1, replica_groups=mesh['seq'=2,'dom'=8,'tm'=2] {'dom'}, use_global_device_ids=true, to_apply=%region_3.4 | all-reduce | flops 1 | bytes 8 | tf_op jit(solution)/shard_map/pmax | solution.py:102
  62.1 1.2 fusion.81
  63.3 16.3 %all-gather = f32[8,96,2]{1,2,0:T(2,128)S(1)} all-gather(f32[1,96,2]{1,2,0:T(2,128)S(1)} %maximum_bitcast_fusion), channel_id=1, replica_groups=mesh['seq'=2,'dom'=8,'tm'=2] {'dom'}, dimensions={0}, use_global_device_ids=true | all-gather | bytes 6912 | tf_op jit(solution)/shard_map/all_gather | solution.py:91
  79.7 1.2 while.98
  79.8 0.3 fusion.143
  80.4 0.3 fusion.143
  81.0 0.6 copy-done.4
  81.7 0.6 dynamic-slice
  83.1 1.2 while.96
  83.2 0.3 fusion.136
  83.7 0.3 fusion.136
  84.3 1.5 while.97
  84.8 0.2 dynamic_update_slice.36
  85.5 0.2 dynamic_update_slice.36
  85.8 19.9 %all-reduce.4 = (f32[768]{0:T(1024)S(1)}, f32[]{:T(128)}) all-reduce(f32[768]{0:T(1024)S(1)} %get-tuple-element.769, f32[]{:T(128)} %get-tuple-element.1041), channel_id=2, replica_groups=mesh['seq'=2,'dom'=8,'tm'=2] {'dom'}, use_global_device_ids=true, to_apply=%region_13.0.clone | all-reduce | flops 769 | bytes 6152
  105.6 1.3 broadcast_select_fusion.5
  106.9 1.5 while.99
  107.4 0.2 dynamic_update_slice.37
  108.1 0.2 dynamic_update_slice.37
  108.4 17.1 %all-reduce.1 = f32[768]{0:T(1024)S(1)} all-reduce(f32[768]{0:T(1024)S(1)} %get-tuple-element.772), channel_id=3, replica_groups=mesh['seq'=2,'dom'=8,'tm'=2] {'dom'}, use_global_device_ids=true, to_apply=%region_21.22.clone | all-reduce | flops 768 | bytes 6144
  125.6 1.3 collective-permute-start.1
  127.2 0.3 fusion.52
  127.5 0.3 fusion.50
  127.8 0.2 fusion.86
  128.1 0.2 convolution_subtract_fusion
  128.3 0.3 fusion.44
  128.7 1.5 while.100
  129.1 0.2 dynamic_update_slice.38
  129.9 0.2 dynamic_update_slice.38
  130.1 19.1 %all-reduce.2 = f32[768]{0:T(1024)S(1)} all-reduce(f32[768]{0:T(1024)S(1)} %get-tuple-element.773), channel_id=4, replica_groups=mesh['seq'=2,'dom'=8,'tm'=2] {'dom'}, use_global_device_ids=true, to_apply=%region_25.26.clone | all-reduce | flops 768 | bytes 6144
  149.3 1.5 while.101
  149.8 0.2 dynamic_update_slice.39
  150.5 0.2 dynamic_update_slice.39
  150.8 17.1 %all-reduce.3 = f32[768]{0:T(1024)S(1)} all-reduce(f32[768]{0:T(1024)S(1)} %get-tuple-element.774), channel_id=5, replica_groups=mesh['seq'=2,'dom'=8,'tm'=2] {'dom'}, use_global_device_ids=true, to_apply=%region_29.30.clone | all-reduce | flops 768 | bytes 6144
  168.3 0.3 fusion.51
  168.6 0.3 fusion.49
  169.2 0.2 convolution_subtract_fusion.2
  169.4 0.9 fusion.48
  170.4 0.6 fusion.80
  170.9 88.0 %all-reduce.7.cloned.1.call-done = f32[128,128]{0,1:T(8,128)} async-done(((f32[128,128]{0,1:T(8,128)}), f32[128,128]{0,1:T(8,128)}) %all-reduce.7.cloned.1.call-update) | async-done | bytes 65552 | tf_op jit(solution)/shard_map/psum | solution.py:154
  258.9 1.6 copy.10
  (86 shorter events, 6.6 us)
Async XLA Ops:
  7.2 30.9 %copy-start = (bf16[128,128]{1,0:T(8,128)(2,1)S(1)}, bf16[128,128]{1,0:T(8,128)(2,1)}, u32[]{:S(2)}) copy-start(bf16[128,128]{1,0:T(8,128)(2,1)} %param.18) | copy-start | bytes 98308
  7.2 2.2 copy-start.1
  7.2 251.7 %all-reduce.7.cloned.1.call-start = ((), (), s32[]{:S(2)}) async-start(), calls=%async_computation | async-start | bytes 131072 | tf_op jit(solution)/shard_map/psum | solution.py:154
  8.0 30.0 %copy-start.2 = (f32[128]{0:T(128)S(1)}, f32[128]{0:T(128)}, u32[]{:S(2)}) copy-start(f32[128]{0:T(128)} %param.19) | copy-start | bytes 1540
  8.0 74.9 %collective-permute-start = (bf16[96,128]{1,0:T(8,128)(2,1)S(1)}, bf16[96,128]{1,0:T(8,128)(2,1)S(1)}, u32[]{:S(2)}, u32[]{:S(2)}) collective-permute-start(bf16[96,128]{1,0:T(8,128)(2,1)S(1)} %slice_bitcast_fusion.2), channel_id=1, source_target_pairs={{1,0},{3,2},{5,4},{7,6},{9,8},{11,10},{13,12},{15,14},{17,16},{19,... | collective-permute-start | bytes 73736 | tf_op jit(solution)/shard_map/ppermute | solution.py:12
  38.7 0.7 copy-start.3
  81.0 0.7 copy-start.4
  125.6 3.0 %collective-permute-start.1 = (f32[96]{0:T(128)S(1)}, f32[96]{0:T(128)S(1)}, u32[]{:S(2)}, u32[]{:S(2)}) collective-permute-start(f32[96]{0:T(128)S(1)} %slice_bitcast_fusion.3), channel_id=1, source_target_pairs={{1,0},{3,2},{5,4},{7,6},{9,8},{11,10},{13,12},{15,14},{17,16},{19,... | collective-permute-start | bytes 1160 | tf_op jit(solution)/shard_map/ppermute | solution.py:12
Sparse Core Ops, SparseCore 0:
  170.5 88.4 all-reduce.6
where the time goes:
time: 268 us; the launch traced here: 267 us
  blocking collectives  140 us (52%)
  waiting for transfers between devices  88.1 us (33%)
  between operations  14.9 us (6%)
  matrix products  8.92 us (3%)
  local copies, waits for them, and re-layouts  7.58 us (3%)
  other arithmetic  4.58 us (2%)
  starting transfers between devices  2.74 us (1%)
    psum x1, waiting for transfers between devices, shards(): score = lax.psum(partial_value, ('dom', 'tm'))  88 us
    unnamed x4, blocking collectives  73.2 us
    all_gather x1, blocking collectives, shards(): whole = lax.all_gather(particles, 'dom', axis=1, tiled=True)  28.6 us
    pmax x1, blocking collectives, shards(): global_top = lax.pmax(jnp.max(final_logs), 'dom')  22.1 us
    all_gather x1, blocking collectives, shards(): full_bias = lax.all_gather(local_bias, 'dom', axis=1, tiled=True)  16.3 us
  transfers between devices with their start and end apart: 3, of which 2 were waited for; matrix products, arithmetic and copies ran while one was open for 2% of the time, Pallas kernels for 0%

commit v1 on v0

--- a/solution.py
+++ b/solution.py
@@ -4,6 +4,28 @@
 from jax.sharding import PartitionSpec as P
 
 exact_mode = lax.Precision.HIGHEST
+
+
+def laid_out(pieces, dim):
+    lengths = list(pieces.shape[1:])
+    lengths[dim] *= pieces.shape[0]
+    return jnp.moveaxis(pieces, 0, dim).reshape(lengths)
+
+
+def collect(shard, axis, dim):
+    size = lax.axis_size(axis)
+    pairs = [(i, (i + 1) % size) for i in range(size)]
+    back = [(b, a) for a, b in pairs]
+    lower, upper = ([], [])
+    for step in range(size - 1):
+        if step % 2 == 0:
+            lower.append(lax.ppermute(lower[-1] if lower else shard, axis, pairs))
+        else:
+            upper.append(lax.ppermute(upper[-1] if upper else shard, axis, back))
+    pieces = jnp.stack([*lower[::-1], shard, *upper])
+    shift = lax.axis_index(axis) - len(lower)
+    pieces = pieces[(jnp.arange(size) - shift) % size]
+    return laid_out(pieces, dim)
 
 
 def from_behind(x, axis, by):
@@ -88,7 +110,7 @@
         predicted = jnp.dot(particles[k], trans_weight.T, preferred_element_type=jnp.float32)
         biases.append(log_weight[k] - 0.5 * jnp.sum(precision * predicted * predicted, axis=1))
     local_bias = jnp.stack(biases)
-    full_bias = lax.all_gather(local_bias, "dom", axis=1, tiled=True)
+    full_bias = collect(local_bias, "dom", 1)
     row_norms = []
     whole = lax.all_gather(particles, "dom", axis=1, tiled=True)
     for k in range(steps_here):

time: 268 us -> 278 us (1.037)
  starting transfers between devices: 2.74 us -> 12.2 us
  waiting for transfers between devices: 88.1 us -> 95.2 us
  blocking collectives: 140 us -> 133 us
    all_gather x1 -> x0, blocking collectives: 16.3 us -> none  [shards(): full_bias = lax.all_gather(local_bias, 'dom', axis=1, tiled=True)]
    ppermute x0 -> x7, starting transfers between devices: none -> 9.59 us  [the longest x3 9.53 us: collect(): upper.append(lax.ppermute(upper[-1] if upper else shard, axis, back))]
    unnamed x4, blocking collectives: 73.2 us -> 80.9 us
    ppermute x0 -> x7, waiting for transfers between devices: none -> 7.14 us  [the longest x4 5.91 us: collect(): lower.append(lax.ppermute(lower[-1] if lower else shard, axis, pairs))]
    all_gather x1, blocking collectives: 28.6 us -> 32.9 us  [shards(): whole = lax.all_gather(particles, 'dom', axis=1, tiled=True)]
  transfers between devices with their start and end apart: 3 -> 10, of which waited for: 2 -> 5; matrix products, arithmetic and copies ran while one was open for 2% -> 2% of each run, Pallas kernels for 0% -> 0%
where the time goes in v1:
time: 278 us
  blocking collectives  133 us (48%)
  waiting for transfers between devices  95.2 us (34%)
  between operations  14.9 us (5%)
  starting transfers between devices  12.2 us (4%)
  matrix products  9.67 us (3%)
  local copies, waits for them, and re-layouts  6.87 us (2%)
  other arithmetic  5.3 us (2%)
    psum x1, waiting for transfers between devices, shards(): score = lax.psum(partial_value, ('dom', 'tm'))  88 us
    unnamed x4, blocking collectives  80.9 us
    all_gather x1, blocking collectives, shards(): whole = lax.all_gather(particles, 'dom', axis=1, tiled=True)  32.9 us
    pmax x1, blocking collectives, shards(): global_top = lax.pmax(jnp.max(final_logs), 'dom')  19.5 us
    ppermute x3, starting transfers between devices, collect(): upper.append(lax.ppermute(upper[-1] if upper else shard, axis, back))  9.53 us
    ppermute x4, waiting for transfers between devices, collect(): lower.append(lax.ppermute(lower[-1] if lower else shard, axis, pairs))  5.91 us
  transfers between devices with their start and end apart: 10, of which 5 were waited for; matrix products, arithmetic and copies ran while one was open for 2% of the time, Pallas kernels for 0%

profile of v1, /device:TPU:8, one launch (start us, length us, event | category | flops | bytes accessed | tf_op | source)
XLA Modules:
  0.0 277.7 jit_solution(5753690974708293607)
XLA Ops:
  7.2 1.3 slice_reduce_fusion.2
  8.5 1.0 fusion.54
  9.6 0.3 fusion.53
  9.8 19.5 %pmax.7 = f32[]{:T(128)} all-reduce(f32[]{:T(128)} %slice_reduce_fusion.2), channel_id=1, replica_groups=mesh['seq'=2,'dom'=8,'tm'=2] {'dom'}, use_global_device_ids=true, to_apply=%region_3.4 | all-reduce | flops 1 | bytes 8 | tf_op jit(solution)/shard_map/pmax | solution.py:124
  29.3 1.2 fusion.83
  30.5 2.9 %collective-permute-start.5 = (f32[2,96]{1,0:T(2,128)S(1)}, f32[2,96]{1,0:T(2,128)S(1)}, u32[]{:S(2)}, u32[]{:S(2)}) collective-permute-start(f32[2,96]{1,0:T(2,128)S(1)} %pad_maximum_fusion), channel_id=1, source_target_pairs={{2,0},{4,2},{6,4},{8,6},{10,8},{12,10},{14,12},{0,14},{3,1},{5,3},... | collective-permute-start | bytes 2312 | tf_op jit(solution)/shard_map/ppermute | solution.py:24
  33.4 1.3 collective-permute-start
  34.7 32.9 %all_gather.3 = bf16[2,768,128]{2,1,0:T(8,128)(2,1)S(1)} all-gather(bf16[2,96,128]{2,1,0:T(8,128)(2,1)S(1)} %copy-done.1), channel_id=1, replica_groups=mesh['seq'=2,'dom'=8,'tm'=2] {'dom'}, dimensions={1}, use_global_device_ids=true | all-gather | bytes 442368 | tf_op jit(solution)/shard_map/all_gather | solution.py:115
  67.9 4.4 %collective-permute-done.2 = f32[2,96]{1,0:T(2,128)S(1)} collective-permute-done((f32[2,96]{1,0:T(2,128)S(1)}, f32[2,96]{1,0:T(2,128)S(1)}, u32[]{:S(2)}, u32[]{:S(2)}) %collective-permute-start.2) | collective-permute-done | bytes 800 | tf_op jit(solution)/shard_map/ppermute | solution.py:22
  72.4 3.0 %collective-permute-start.6 = (f32[2,96]{1,0:T(2,128)S(1)}, f32[2,96]{1,0:T(2,128)S(1)}, u32[]{:S(2)}, u32[]{:S(2)}) collective-permute-start(f32[2,96]{1,0:T(2,128)S(1)} %collective-permute-done.5), channel_id=1, source_target_pairs={{2,0},{4,2},{6,4},{8,6},{10,8},{12,10},{14,12},{0,14},{3,1},{5,3},... | collective-permute-start | bytes 2312 | tf_op jit(solution)/shard_map/ppermute | solution.py:24
  75.3 1.5 collective-permute-done.3
  76.8 0.7 copy-done.4
  77.5 0.6 dynamic-slice
  78.6 3.7 %collective-permute-start.7 = (f32[2,96]{1,0:T(2,128)S(1)}, f32[2,96]{1,0:T(2,128)S(1)}, u32[]{:S(2)}, u32[]{:S(2)}) collective-permute-start(f32[2,96]{1,0:T(2,128)S(1)} %collective-permute-done.6), channel_id=1, source_target_pairs={{2,0},{4,2},{6,4},{8,6},{10,8},{12,10},{14,12},{0,14},{3,1},{5,3},... | collective-permute-start | bytes 2312 | tf_op jit(solution)/shard_map/ppermute | solution.py:24
  82.4 1.2 collective-permute-done.7
  83.6 0.6 gather_fusion
  84.3 1.2 while.98
  84.4 0.3 fusion.145
  85.0 0.3 fusion.145
  85.7 1.2 while.96
  85.8 0.3 fusion.138
  86.4 0.3 fusion.138
  86.9 1.5 while.97
  87.4 0.2 dynamic_update_slice.36
  88.2 0.2 dynamic_update_slice.36
  88.4 27.5 %all-reduce.4 = (f32[768]{0:T(1024)S(1)}, f32[]{:T(128)}) all-reduce(f32[768]{0:T(1024)S(1)} %get-tuple-element.769, f32[]{:T(128)} %get-tuple-element.1039), channel_id=2, replica_groups=mesh['seq'=2,'dom'=8,'tm'=2] {'dom'}, use_global_device_ids=true, to_apply=%region_13.14.clone | all-reduce | flops 769 | bytes 6152
  116.0 1.3 broadcast_select_fusion.5
  117.2 1.5 while.99
  117.7 0.2 dynamic_update_slice.37
  118.4 0.2 dynamic_update_slice.37
  118.7 17.1 %all-reduce.1 = f32[768]{0:T(1024)S(1)} all-reduce(f32[768]{0:T(1024)S(1)} %get-tuple-element.772), channel_id=3, replica_groups=mesh['seq'=2,'dom'=8,'tm'=2] {'dom'}, use_global_device_ids=true, to_apply=%region_21.22.clone | all-reduce | flops 768 | bytes 6144
  136.0 1.3 collective-permute-start.8
  137.5 0.3 fusion.52
  137.8 0.3 fusion.50
  138.7 0.3 fusion.44
  139.0 1.5 while.100
  139.5 0.2 dynamic_update_slice.38
  140.2 0.2 dynamic_update_slice.38
  140.5 19.1 %all-reduce.2 = f32[768]{0:T(1024)S(1)} all-reduce(f32[768]{0:T(1024)S(1)} %get-tuple-element.773), channel_id=4, replica_groups=mesh['seq'=2,'dom'=8,'tm'=2] {'dom'}, use_global_device_ids=true, to_apply=%region_25.26.clone | all-reduce | flops 768 | bytes 6144
  159.6 1.5 while.101
  160.1 0.2 dynamic_update_slice.39
  161.1 17.1 %all-reduce.3 = f32[768]{0:T(1024)S(1)} all-reduce(f32[768]{0:T(1024)S(1)} %get-tuple-element.774), channel_id=5, replica_groups=mesh['seq'=2,'dom'=8,'tm'=2] {'dom'}, use_global_device_ids=true, to_apply=%region_29.30.clone | all-reduce | flops 768 | bytes 6144
  178.6 0.3 fusion.51
  178.9 0.3 fusion.49
  179.8 0.9 fusion.48
  180.7 0.6 fusion.80
  181.3 88.0 %all-reduce.7.cloned.1.call-done = f32[128,128]{0,1:T(8,128)} async-done(((f32[128,128]{0,1:T(8,128)}), f32[128,128]{0,1:T(8,128)}) %all-reduce.7.cloned.1.call-update) | async-done | bytes 65552 | tf_op jit(solution)/shard_map/psum | solution.py:176
  269.3 1.6 copy.7
  (110 shorter events, 7.9 us)
Async XLA Ops:
  7.2 1.4 copy-start
  7.2 2.4 copy-start.1
  7.2 262.1 %all-reduce.7.cloned.1.call-start = ((), (), s32[]{:S(2)}) async-start(), calls=%async_computation | async-start | bytes 131072 | tf_op jit(solution)/shard_map/psum | solution.py:176
  8.5 1.0 copy-start.2
  9.8 19.5 %copy-start.3 = (f32[2,96]{1,0:T(2,128)S(1)}, f32[2,96]{1,0:T(2,128)}, u32[]{:S(2)}) copy-start(f32[2,96]{1,0:T(2,128)} %param.17) | copy-start | bytes 2308
  30.5 37.3 %collective-permute-start.1 = (f32[2,96]{1,0:T(2,128)S(1)}, f32[2,96]{1,0:T(2,128)S(1)}, u32[]{:S(2)}, u32[]{:S(2)}) collective-permute-start(f32[2,96]{1,0:T(2,128)S(1)} %pad_maximum_fusion), channel_id=1, source_target_pairs={{0,2},{2,4},{4,6},{6,8},{8,10},{10,12},{12,14},{14,0},{1,3},{3,5},... | collective-permute-start | bytes 2312 | tf_op jit(solution)/shard_map/ppermute | solution.py:22
  30.5 41.9 %collective-permute-start.5 = (f32[2,96]{1,0:T(2,128)S(1)}, f32[2,96]{1,0:T(2,128)S(1)}, u32[]{:S(2)}, u32[]{:S(2)}) collective-permute-start(f32[2,96]{1,0:T(2,128)S(1)} %pad_maximum_fusion), channel_id=1, source_target_pairs={{2,0},{4,2},{6,4},{8,6},{10,8},{12,10},{14,12},{0,14},{3,1},{5,3},... | collective-permute-start | bytes 2312 | tf_op jit(solution)/shard_map/ppermute | solution.py:24
  33.4 52.1 %collective-permute-start = (bf16[96,128]{1,0:T(8,128)(2,1)S(1)}, bf16[96,128]{1,0:T(8,128)(2,1)S(1)}, u32[]{:S(2)}, u32[]{:S(2)}) collective-permute-start(bf16[96,128]{1,0:T(8,128)(2,1)S(1)} %slice_bitcast_fusion.2), channel_id=1, source_target_pairs={{1,0},{3,2},{5,4},{7,6},{9,8},{11,10},{13,12},{15,14},{17,16},{19,... | collective-permute-start | bytes 73736 | tf_op jit(solution)/shard_map/ppermute | solution.py:34
  67.8 4.5 %collective-permute-start.2 = (f32[2,96]{1,0:T(2,128)S(1)}, f32[2,96]{1,0:T(2,128)S(1)}, u32[]{:S(2)}, u32[]{:S(2)}) collective-permute-start(f32[2,96]{1,0:T(2,128)S(1)} %collective-permute-done.1), channel_id=1, source_target_pairs={{0,2},{2,4},{4,6},{6,8},{8,10},{10,12},{12,14},{14,0},{1,3},{3,5},... | collective-permute-start | bytes 2312 | tf_op jit(solution)/shard_map/ppermute | solution.py:22
  72.4 4.5 %collective-permute-start.3 = (f32[2,96]{1,0:T(2,128)S(1)}, f32[2,96]{1,0:T(2,128)S(1)}, u32[]{:S(2)}, u32[]{:S(2)}) collective-permute-start(f32[2,96]{1,0:T(2,128)S(1)} %collective-permute-done.2), channel_id=1, source_target_pairs={{0,2},{2,4},{4,6},{6,8},{8,10},{10,12},{12,14},{14,0},{1,3},{3,5},... | collective-permute-start | bytes 2312 | tf_op jit(solution)/shard_map/ppermute | solution.py:22
  72.4 6.2 %collective-permute-start.6 = (f32[2,96]{1,0:T(2,128)S(1)}, f32[2,96]{1,0:T(2,128)S(1)}, u32[]{:S(2)}, u32[]{:S(2)}) collective-permute-start(f32[2,96]{1,0:T(2,128)S(1)} %collective-permute-done.5), channel_id=1, source_target_pairs={{2,0},{4,2},{6,4},{8,6},{10,8},{12,10},{14,12},{0,14},{3,1},{5,3},... | collective-permute-start | bytes 2312 | tf_op jit(solution)/shard_map/ppermute | solution.py:24
  76.8 5.5 %collective-permute-start.4 = (f32[2,96]{1,0:T(2,128)S(1)}, f32[2,96]{1,0:T(2,128)S(1)}, u32[]{:S(2)}, u32[]{:S(2)}) collective-permute-start(f32[2,96]{1,0:T(2,128)S(1)} %collective-permute-done.3), channel_id=1, source_target_pairs={{0,2},{2,4},{4,6},{6,8},{8,10},{10,12},{12,14},{14,0},{1,3},{3,5},... | collective-permute-start | bytes 2312 | tf_op jit(solution)/shard_map/ppermute | solution.py:22
  76.8 0.7 copy-start.4
  78.6 5.0 %collective-permute-start.7 = (f32[2,96]{1,0:T(2,128)S(1)}, f32[2,96]{1,0:T(2,128)S(1)}, u32[]{:S(2)}, u32[]{:S(2)}) collective-permute-start(f32[2,96]{1,0:T(2,128)S(1)} %collective-permute-done.6), channel_id=1, source_target_pairs={{2,0},{4,2},{6,4},{8,6},{10,8},{12,10},{14,12},{0,14},{3,1},{5,3},... | collective-permute-start | bytes 2312 | tf_op jit(solution)/shard_map/ppermute | solution.py:24
  136.0 3.0 %collective-permute-start.8 = (f32[96]{0:T(128)S(1)}, f32[96]{0:T(128)S(1)}, u32[]{:S(2)}, u32[]{:S(2)}) collective-permute-start(f32[96]{0:T(128)S(1)} %slice_bitcast_fusion.3), channel_id=1, source_target_pairs={{1,0},{3,2},{5,4},{7,6},{9,8},{11,10},{13,12},{15,14},{17,16},{19,... | collective-permute-start | bytes 1160 | tf_op jit(solution)/shard_map/ppermute | solution.py:34
Sparse Core Ops, SparseCore 0:
  180.8 88.4 all-reduce.6
